TPU v7x, 256 devices: a whole 4x4x8 slice. The times are simulated.
256 devices in a mesh: row: 32 (over x, y, core), col: 8 (over z).
Axes of the slice: x: 4, y: 4, z: 8, core: 2. Of those that a mesh axis runs over, the one named last changes fastest.
Arguments:
- kernel: float32 [4, 4096, 16, 1024], P(None, 'row', None, 'col'), as said below
Outputs:
- factored: float32 [4, 4096, 16, 1024], P(None, 'row', None, 'col')
Inputs may be any that keep to these rules, and one draw needn't show every extreme that they name: kernel is symmetric and positive definite.
All inputs are finite; a program needn't handle non-finite values.
Results may differ from a plain program's by a relative error of at most 0.0001.
Values sent between devices are 32-bit elements; how exact they have to be, the bound alone decides.
A program may use at most 128 MiB of HBM per device.

v0:
```python
import jax
import jax.numpy as jnp
from jax import lax
from jax.sharding import PartitionSpec as P

PANELS = 2


def from_root(value, axis, source):
    kept = jnp.where(lax.axis_index(axis) == source, value, 0).astype(value.dtype)
    return lax.psum(kept, axis)


def solve_panel(column, panel_idx, grid_row, spread):
    blocks = column.shape[0]
    breadth = column.shape[1]
    diagonal = from_root(column[0], "row", panel_idx)
    factor = jnp.linalg.cholesky(diagonal)
    stacked = column.reshape(blocks * breadth, breadth)
    solved = jax.scipy.linalg.solve_triangular(factor, stacked.T, lower=True).T
    solved = solved.reshape(blocks, breadth, breadth)
    global_rows = jnp.arange(blocks, dtype=jnp.int32) * spread + grid_row
    solved = jnp.where((global_rows < panel_idx)[:, None, None], jnp.float32(0.0), solved)
    solved = jnp.where((global_rows == panel_idx)[:, None, None], factor[None], solved)
    return from_root(solved, "col", panel_idx)


def mirror(rows_part, grid_col):
    n_row = lax.axis_size("row")
    n_col = lax.axis_size("col")
    local_rows = rows_part.shape[0]
    breadth = rows_part.shape[1]
    extent = rows_part.shape[2]
    whole = lax.all_gather(rows_part, "row", axis=1, tiled=True)
    whole = whole.reshape(local_rows * n_row // n_col, n_col, breadth, extent)
    return lax.dynamic_index_in_dim(whole, grid_col, 1, keepdims=False)


def trailing(matrix, row_panel, col_panel):
    update = jnp.einsum("rib,cjb->ricj", row_panel, col_panel, precision=lax.Precision.HIGHEST)
    return matrix - update


def settle(matrix, panel_rows, panel_idx, global_rows, global_cols):
    col_mask = (global_cols == panel_idx)[None, None, :, None]
    matrix = jnp.where(col_mask, panel_rows[:, :, None, :], matrix)
    row_mask = (global_rows == panel_idx)[:, None, None, None] & (global_cols > panel_idx)[
        None, None, :, None
    ]
    return jnp.where(row_mask, jnp.float32(0.0), matrix)


def shards(kernel):
    grid_row = lax.axis_index("row")
    grid_col = lax.axis_index("col")
    n_row = lax.axis_size("row")
    n_col = lax.axis_size("col")
    global_rows = jnp.arange(kernel.shape[0], dtype=jnp.int32) * n_row + grid_row
    global_cols = jnp.arange(kernel.shape[2], dtype=jnp.int32) * n_col + grid_col
    matrix = kernel
    for panel_idx in range(PANELS):
        current = solve_panel(matrix[:, :, 0, :], panel_idx, grid_row, n_row)
        matrix = trailing(matrix, current, mirror(current, grid_col))
        matrix = settle(matrix, current, panel_idx, global_rows, global_cols)
    return matrix


def solution(mesh):
    in_specs = (P(None, "row", None, "col"),)
    out_specs = P(None, "row", None, "col")
    return jax.shard_map(shards, mesh=mesh, in_specs=in_specs, out_specs=out_specs, check_vma=False)
```

profile of v0, /device:TPU:128, one launch (start us, length us, event | category | flops | bytes accessed | tf_op | source)
XLA Modules:
  0.0 568.9 jit_solution(5533761548041948064)
XLA Ops:
  6.5 5.3 copy.14
  11.8 1.5 fusion.7
  13.4 1.7 slice.25
  15.1 105.7 %all-reduce.5.cloned.1.call-done = f32[128,128]{0,1:T(8,128)} async-done(((f32[128,128]{0,1:T(8,128)}), f32[128,128]{0,1:T(8,128)}) %all-reduce.5.cloned.1.call-update) | async-done | bytes 65552 | tf_op jit(solution)/shard_map/psum | solution.py:11
  120.8 0.9 copy.15
  121.8 0.9 fusion.11
  122.6 11.7 %cholesky.44 = f32[128,128]{1,0:T(8,128)S(1)} custom-call(f32[128,128]{1,0:T(8,128)S(1)} %fusion.11), custom_call_target="Cholesky" | custom-call | tf_op jit(solution)/shard_map/jit(cholesky)/cholesky | solution.py:18
  135.6 9.8 %custom-call.6 = f32[1,128,128]{1,2,0:T(8,128)S(1)} custom-call(f32[1,128,128]{2,1,0:T(8,128)S(1)} %get-tuple-element.9), custom_call_target="InvertDiagBlocksLowerTriangular" | custom-call | tf_op jit(solution)/shard_map/jit(_solve_triangular)/triangular_solve | solution.py:20
  146.8 68.6 %all-reduce.7.cloned.1.call-done = f32[4,128,128]{2,1,0:T(8,128)} async-done(((f32[4,128,128]{2,1,0:T(8,128)}), f32[4,128,128]{2,1,0:T(8,128)}) %all-reduce.7.cloned.1.call-update) | async-done | bytes 262160 | tf_op jit(solution)/shard_map/psum | solution.py:11
  215.6 1.1 copy.17
  216.7 60.7 %all-gather.3.cloned.1.call-done = f32[4,4096,128]{2,1,0:T(8,128)} async-done(((f32[4,128,128]{2,1,0:T(8,128)}), f32[4,4096,128]{2,1,0:T(8,128)}) %all-gather.3.cloned.1.call-update) | async-done | bytes 8388624 | tf_op jit(solution)/shard_map/all_gather | solution.py:34
  277.4 6.4 %select_select_fusion.1 = f32[4,128,16,128]{1,3,2,0:T(8,128)S(1)} fusion(f32[4,128,16,128]{1,3,2,0:T(8,128)} %copy.14, f32[4,128,128]{1,2,0:T(8,128)S(1)} %copy.17, pred[16]{0:T(512)(128)(4,1)S(1)} %get-tuple-element.13, pred[4,16]{1,0:T(4,128)(4,1)S(1)} %broadcast_and_fusion, f32[16,8,128,128]{3,2,1,0:T(8,128)} %bitcast.62, s32[]{:T(128)S(6)} %select_n.79, ...), kind=kOutput, calls=%fused_computation.1 | convolution fusion | flops 1613758464 | bytes 9961556 | tf_op jit(solution)/shard_map/rib,cjb->ricj/dot_general | solution.py:40
  283.8 2.0 copy-done
  286.7 1.0 slice.30
  287.8 104.2 %all-reduce.9.cloned.1.call-done = f32[128,128]{0,1:T(8,128)} async-done(((f32[128,128]{0,1:T(8,128)}), f32[128,128]{0,1:T(8,128)}) %all-reduce.9.cloned.1.call-update) | async-done | bytes 65552 | tf_op jit(solution)/shard_map/psum | solution.py:11
  392.1 0.9 copy.21
  393.0 0.9 fusion.9
  393.8 11.7 %cholesky.55 = f32[128,128]{1,0:T(8,128)S(1)} custom-call(f32[128,128]{1,0:T(8,128)S(1)} %fusion.9), custom_call_target="Cholesky" | custom-call | tf_op jit(solution)/shard_map/jit(cholesky)/cholesky | solution.py:18
  406.8 9.8 %custom-call.7 = f32[1,128,128]{1,2,0:T(8,128)S(1)} custom-call(f32[1,128,128]{2,1,0:T(8,128)S(1)} %get-tuple-element.6), custom_call_target="InvertDiagBlocksLowerTriangular" | custom-call | tf_op jit(solution)/shard_map/jit(_solve_triangular)/triangular_solve | solution.py:20
  418.0 68.6 %all-reduce.11.cloned.1.call-done = f32[4,128,128]{2,1,0:T(8,128)} async-done(((f32[4,128,128]{2,1,0:T(8,128)}), f32[4,128,128]{2,1,0:T(8,128)}) %all-reduce.11.cloned.1.call-update) | async-done | bytes 262160 | tf_op jit(solution)/shard_map/psum | solution.py:11
  486.7 1.1 copy.24
  487.8 60.6 %all-gather.5.cloned.1.call-done = f32[4,4096,128]{2,1,0:T(8,128)} async-done(((f32[4,128,128]{2,1,0:T(8,128)}), f32[4,4096,128]{2,1,0:T(8,128)}) %all-gather.5.cloned.1.call-update) | async-done | bytes 8388624 | tf_op jit(solution)/shard_map/all_gather | solution.py:34
  548.4 8.2 %select_select_fusion = f32[4,128,16,128]{1,3,2,0:T(8,128)} fusion(f32[4,128,16,128]{1,3,2,0:T(8,128)} %copy-done, f32[4,128,128]{1,2,0:T(8,128)S(1)} %copy.24, pred[16]{0:T(512)(128)(4,1)S(1)} %get-tuple-element.15, pred[4,16]{1,0:T(4,128)(4,1)S(1)} %broadcast_and_fusion.1, f32[16,8,128,128]{3,2,1,0:T(8,128)} %bitcast.63, s32[]{:T(128)S(6)} %select_n.79, ...), kind=kOutput, calls=%fused_computation | convolution fusion | flops 1613758464 | bytes 9961556 | tf_op jit(solution)/shard_map/rib,cjb->ricj/dot_general | solution.py:40
  556.7 5.4 copy.26
  (34 shorter events, 6.6 us)
Async XLA Ops:
  6.5 114.3 %all-reduce.5.cloned.1.call-start = ((), (), s32[]{:S(2)}) async-start(), calls=%async_computation | async-start | bytes 131072 | tf_op jit(solution)/shard_map/psum | solution.py:11
  13.3 202.1 %all-reduce.7.cloned.1.call-start = ((), (), s32[]{:S(2)}) async-start(), calls=%async_computation.1 | async-start | bytes 524288 | tf_op jit(solution)/shard_map/psum | solution.py:11
  146.8 130.6 %all-gather.3.cloned.1.call-start = ((), (), s32[]{:S(2)}) async-start(), calls=%async_computation.2 | async-start | bytes 8650752 | tf_op jit(solution)/shard_map/all_gather | solution.py:34
  215.5 176.6 %all-reduce.9.cloned.1.call-start = ((), (), s32[]{:S(2)}) async-start(), calls=%async_computation.3 | async-start | bytes 131072 | tf_op jit(solution)/shard_map/psum | solution.py:11
  283.8 2.0 copy-start
  286.5 200.1 %all-reduce.11.cloned.1.call-start = ((), (), s32[]{:S(2)}) async-start(), calls=%async_computation.4 | async-start | bytes 524288 | tf_op jit(solution)/shard_map/psum | solution.py:11
  418.0 130.4 %all-gather.5.cloned.1.call-start = ((), (), s32[]{:S(2)}) async-start(), calls=%async_computation.5 | async-start | bytes 8650752 | tf_op jit(solution)/shard_map/all_gather | solution.py:34
Sparse Core Ops, SparseCore 0:
  13.4 107.3 all-reduce.4
  146.9 68.4 all-reduce.6
  218.1 59.2 all-gather.2
  286.6 105.4 all-reduce.8
  418.1 68.4 all-reduce.10
  489.1 59.2 all-gather.4
where the time goes:
time: 572 us; the launch traced here: 569 us
  waiting for transfers between devices  469 us (82%)
  other arithmetic  51.1 us (9%)
  local copies, waits for them, and re-layouts  19.8 us (3%)
  matrix products  15.5 us (3%)
  between operations  13.7 us (2%)
    psum x4, waiting for transfers between devices, from_root(): return lax.psum(kept, axis)  347 us
    all_gather x2, waiting for transfers between devices, mirror(): whole = lax.all_gather(rows_part, 'row', axis=1, tiled=True)  121 us
    another operation x6, other arithmetic, solve_panel(): factor = jnp.linalg.cholesky(diagonal)  24.8 us
    another operation x4, other arithmetic, solve_panel(): solved = jax.scipy.linalg.solve_triangular(factor, stacked.T, lower=True).T  20.8 us
    dot_general x2, matrix products, trailing(): jnp.einsum('rib,cjb->ricj', row_panel, col_panel, precision=lax.Precision...  14.6 us
  transfers between devices with their start and end apart: 6, of which 6 were waited for; matrix products, arithmetic and copies ran while one was open for 1% of the time, Pallas kernels for 0%

commit v1 on v0

v1 whole, which is shorter than its diff:
```python
import jax
import jax.numpy as jnp
from jax import lax
from jax.experimental import pallas as pl
from jax.experimental.pallas import tpu as pltpu
from jax.sharding import PartitionSpec as P

NX, NY, NZ = 4, 4, 8
BS = 128
GROUP = 8
GROUPS = BS // GROUP
QUARTERS = 4
PIECES = 4
MESH = pl.DeviceIdType.MESH


def dot_nn(a, b):
    return lax.dot_general(
        a,
        b,
        (((1,), (0,)), ((), ())),
        precision=lax.Precision.HIGHEST,
        preferred_element_type=jnp.float32,
    )


def dot_nt(a, b):
    return lax.dot_general(
        a,
        b,
        (((1,), (1,)), ((), ())),
        precision=lax.Precision.HIGHEST,
        preferred_element_type=jnp.float32,
    )


def lane(value, index):
    return jnp.broadcast_to(value[:, index : index + 1], (GROUP, BS))


def factor_block(block, upper_ref, inverse_ref, hook):
    rows = lax.broadcasted_iota(jnp.int32, (GROUP, BS), 0)
    cols = lax.broadcasted_iota(jnp.int32, (GROUP, BS), 1)
    left = [block[GROUP * g : GROUP * (g + 1), :] for g in range(GROUPS)]
    right = [jnp.where(cols == rows + GROUP * g, 1.0, 0.0).astype(jnp.float32) for g in range(GROUPS)]
    for k in range(GROUPS):
        hook(k)
        base = GROUP * k
        r = [jnp.broadcast_to(left[k][i : i + 1, :], (GROUP, BS)) for i in range(GROUP)]
        q = [jnp.broadcast_to(right[k][i : i + 1, :], (GROUP, BS)) for i in range(GROUP)]
        d = [[lane(r[i], base + j) if j <= i else None for j in range(GROUP)] for i in range(GROUP)]
        c = [[lane(left[g], base + p) for p in range(GROUP)] for g in range(k + 1, GROUPS)]
        inv = [None] * GROUP
        for p in range(GROUP):
            inv[p] = lax.rsqrt(d[p][p])
            for i in range(p + 1, GROUP):
                d[i][p] = d[i][p] * inv[p]
            r[p] = r[p] * inv[p]
            q[p] = q[p] * inv[p]
            for i in range(p + 1, GROUP):
                for j in range(p + 1, i + 1):
                    d[i][j] = d[i][j] - d[i][p] * d[j][p]
                r[i] = r[i] - d[i][p] * r[p]
                q[i] = q[i] - d[i][p] * q[p]
            if k + 1 < GROUPS:
                first = c[0]
                first[p] = first[p] * inv[p]
                for j in range(p + 1, GROUP):
                    first[j] = first[j] - first[p] * d[j][p]
                left[k + 1] = left[k + 1] - first[p] * r[p]
                right[k + 1] = right[k + 1] - first[p] * q[p]
        for p in range(GROUP):
            at = base + p
            upper_ref[at : at + 1, :] = jnp.where(cols[0:1] >= at, r[p][0:1], 0.0)
            inverse_ref[at : at + 1, :] = q[p][0:1]
        if k + 2 < GROUPS:
            v = [None] * GROUP
            w = [None] * GROUP
            for p in range(GROUP - 1, -1, -1):
                a, b = r[p], q[p]
                for s in range(p + 1, GROUP):
                    a = a - d[s][p] * v[s]
                    b = b - d[s][p] * w[s]
                v[p] = a * inv[p]
                w[p] = b * inv[p]
            for g in range(k + 2, GROUPS):
                mult = c[g - k - 1]
                for p in range(GROUP):
                    left[g] = left[g] - mult[p] * v[p]
                    right[g] = right[g] - mult[p] * w[p]


def remote(src, dst, send, recv, target):
    return pltpu.make_async_remote_copy(
        src_ref=src, dst_ref=dst, send_sem=send, recv_sem=recv, device_id=target, device_id_type=MESH
    )


def panels_kernel(
    a_ref,
    pr_ref,
    pc_ref,
    cbuf,
    rbuf,
    corner,
    upper,
    inverse,
    load_c,
    load_r,
    r_send,
    r_recv,
    k_send,
    k_recv,
    c_send,
    c_recv,
):
    grid_row = lax.axis_index("row")
    z = lax.axis_index("col")
    core = lax.rem(grid_row, 2)
    y = lax.rem(grid_row // 2, NY)
    x = grid_row // (2 * NY)

    def at(i, j, core_, z_):
        return ((lax.rem(i, NX) * NY + lax.rem(j, NY)) * 2 + core_, lax.rem(z_, NZ))

    sibling = at(x, y, 1 - core, z)
    root = (x == 0) & (y == 0)
    mine = pl.multiple_of(core * BS, BS)

    def c_load(j):
        return pltpu.make_async_copy(
            a_ref.at[0, :, j, :], cbuf.at[pl.ds(mine, BS), pl.ds(j * BS, BS)], load_c.at[j]
        )

    def r_load(panel, i):
        return pltpu.make_async_copy(a_ref.at[i, :, 0, :], rbuf.at[panel, i], load_r.at[i])

    for panel in range(2):

        @pl.when(z == panel)
        def _():
            for i in range(4):
                r_load(panel, i).start()

    @pl.when(root)
    def _():
        for j in range(16):
            c_load(j).start()

    barrier = pltpu.get_barrier_semaphore()
    near = [at(x + m, y, core, z) for m in range(1, NX)]
    near += [at(x, y + m, core, z) for m in range(1, NY)]
    near += [at(x, y, core, z + 1), at(x, y, core, z + NZ - 1), sibling]
    for target in near:
        pl.semaphore_signal(barrier, inc=1, device_id=target, device_id_type=MESH)
    pl.semaphore_wait(barrier, len(near))

    def r_copy(panel, i, up):
        step = 1 if up else NZ - 1
        return remote(
            rbuf.at[panel, i],
            rbuf.at[panel, i],
            r_send.at[panel, i, 0 if up else 1],
            r_recv.at[panel, i],
            at(x, y, core, z + step),
        )

    def r_where(panel):
        rel = lax.rem(z + NZ - panel, NZ)
        return rel == 0, rel <= 3, (rel == 0) | (rel >= 6)

    def r_relay(panel, i):
        first, up, down = r_where(panel)

        @pl.when(first)
        def _():
            r_load(panel, i).wait()

        @pl.when(jnp.logical_not(first))
        def _():
            r_copy(panel, i, True).wait_recv()

        @pl.when(up)
        def _():
            r_copy(panel, i, True).start()

        @pl.when(down)
        def _():
            r_copy(panel, i, False).start()

    def r_finish(panel, i):
        _, up, down = r_where(panel)

        @pl.when(up)
        def _():
            r_copy(panel, i, True).wait_send()

        @pl.when(down)
        def _():
            r_copy(panel, i, False).wait_send()

    owners = (0, 1, 1)
    sources = ((0, 0), (0, 0), (1, 0))

    def k_copy(block, slot, target):
        return remote(corner.at[block], corner.at[block], k_send.at[block, slot], k_recv.at[block], target)

    def k_relay(block):
        owner = core == owners[block]

        @pl.when(owner & root)
        def _():
            corner[block] = rbuf[sources[block]]
            for m in range(1, NX):
                k_copy(block, m - 1, at(x + m, y, core, z)).start()

        @pl.when(jnp.logical_not(owner & root))
        def _():
            k_copy(block, 0, sibling).wait_recv()

        @pl.when(owner & (y == 0))
        def _():
            for m in range(1, NY):
                k_copy(block, NX - 2 + m, at(x, y + m, core, z)).start()

        @pl.when(owner)
        def _():
            k_copy(block, NX + NY - 2, sibling).start()

    def k_finish(block):
        owner = core == owners[block]

        @pl.when(owner & root)
        def _():
            for m in range(1, NX):
                k_copy(block, m - 1, at(x + m, y, core, z)).wait_send()

        @pl.when(owner & (y == 0))
        def _():
            for m in range(1, NY):
                k_copy(block, NX - 2 + m, at(x, y + m, core, z)).wait_send()

        @pl.when(owner)
        def _():
            k_copy(block, NX + NY - 2, sibling).wait_send()

    def c_where(quarter):
        flip = quarter % 2
        a, b = (x, y) if quarter < 2 else (y, x)
        if flip:
            a, b = lax.rem(NX - a, NX), lax.rem(NY - b, NY)
        step = NX - 1 if flip else 1
        along, across = ((step, 0), (0, step)) if quarter < 2 else ((0, step), (step, 0))
        send_along = ((b == 0) & (a < 3)) | ((b > 0) & (a == 3))
        send_across = (a > 0) & (b < 3)
        return (
            send_along,
            at(x + along[0], y + along[1], core, z),
            send_across,
            at(x + across[0], y + across[1], core, z),
        )

    def c_rows(quarter, piece, base):
        height = BS // QUARTERS // PIECES
        return pl.ds(pl.multiple_of(base + (quarter * PIECES + piece) * height, height), height)

    def c_copy(quarter, piece, slot, target):
        view = cbuf.at[c_rows(quarter, piece, mine)]
        return remote(view, view, c_send.at[quarter, piece, slot], c_recv.at[quarter, piece, 0], target)

    def c_pair(quarter, piece):
        view = cbuf.at[c_rows(quarter, piece, mine)]
        return remote(view, view, c_send.at[quarter, piece, 2], c_recv.at[quarter, piece, 1], sibling)

    def c_pair_in(quarter, piece):
        view = cbuf.at[c_rows(quarter, piece, BS - mine)]
        return remote(view, view, c_send.at[quarter, piece, 2], c_recv.at[quarter, piece, 1], sibling)

    def c_relay(quarter, piece):
        send_along, along, send_across, across = c_where(quarter)

        @pl.when(jnp.logical_not(root))
        def _():
            c_copy(quarter, piece, 0, sibling).wait_recv()

        @pl.when(send_along)
        def _():
            c_copy(quarter, piece, 0, along).start()

        @pl.when(send_across)
        def _():
            c_copy(quarter, piece, 1, across).start()

        c_pair(quarter, piece).start()

    def c_finish(quarter, piece):
        send_along, along, send_across, across = c_where(quarter)

        @pl.when(send_along)
        def _():
            c_copy(quarter, piece, 0, along).wait_send()

        @pl.when(send_across)
        def _():
            c_copy(quarter, piece, 1, across).wait_send()

        c_pair(quarter, piece).wait_send()

    r_relay(0, 0)
    k_relay(0)
    r_relay(1, 0)
    k_relay(1)
    k_relay(2)

    @pl.when(root)
    def _():
        for j in range(16):
            c_load(j).wait()

    events = []
    for piece in range(PIECES):
        for quarter in range(QUARTERS):
            events.append((c_relay, quarter, piece))
        if piece < 3:
            events.append((r_relay, 0, piece + 1))
            events.append((r_relay, 1, piece + 1))
    pending = list(events)

    def run(count):
        for _ in range(count):
            if pending:
                f, i, j = pending.pop(0)
                f(i, j)

    factor_block(corner[0], upper.at[0], inverse.at[0], lambda k: run(1))
    below = dot_nt(corner[1], inverse[0])
    second = corner[2] - dot_nt(below, below)
    factor_block(second, upper.at[1], inverse.at[1], lambda k: run(1))
    run(len(pending))

    for i in range(4):
        first_rows = dot_nt(rbuf[0, i], inverse[0])
        pr_ref[i, :, 0:BS] = first_rows
        pr_ref[i, :, BS : 2 * BS] = dot_nt(rbuf[1, i] - dot_nt(first_rows, below), inverse[1])

    @pl.when(grid_row == 0)
    def _():
        pr_ref[0, :, 0:BS] = upper[0].T
        pr_ref[0, :, BS : 2 * BS] = jnp.zeros((BS, BS), jnp.float32)

    @pl.when(grid_row == 1)
    def _():
        pr_ref[0, :, BS : 2 * BS] = upper[1].T

    for quarter in range(QUARTERS):
        for piece in range(PIECES):
            c_pair_in(quarter, piece).wait_recv()
    for j in range(4):
        part = pl.ds(j * 512, 512)
        top = dot_nn(inverse[0], cbuf[0:BS, part])
        pc_ref[0:BS, part] = top
        pc_ref[BS : 2 * BS, part] = dot_nn(inverse[1], cbuf[BS : 2 * BS, part] - dot_nn(below, top))

    for i in range(4):
        for panel in range(2):
            r_finish(panel, i)
    for block in range(3):
        k_finish(block)
    for quarter in range(QUARTERS):
        for piece in range(PIECES):
            c_finish(quarter, piece)


def update_kernel(a_ref, pr_ref, pc_ref, out_ref):
    step = pl.program_id(0)
    grid_row = lax.axis_index("row")
    z = lax.axis_index("col")
    top = (step == 0) & (grid_row < 2)

    @pl.when(top)
    def _():
        out_ref[...] = jnp.zeros_like(out_ref)

    @pl.when(jnp.logical_not(top))
    def _():
        for j in range(16):
            out_ref[0, :, j, :] = a_ref[0, :, j, :] - dot_nn(pr_ref[0], pc_ref[:, j * BS : (j + 1) * BS])

    @pl.when(z == 0)
    def _():
        out_ref[0, :, 0, :] = pr_ref[0, :, 0:BS]

    @pl.when(z == 1)
    def _():
        out_ref[0, :, 0, :] = pr_ref[0, :, BS : 2 * BS]


def shards(kernel):
    f32 = jnp.float32
    pr, pc = pl.pallas_call(
        panels_kernel,
        out_shape=[jax.ShapeDtypeStruct((4, BS, 2 * BS), f32), jax.ShapeDtypeStruct((2 * BS, 16 * BS), f32)],
        in_specs=[pl.BlockSpec(memory_space=pl.ANY)],
        out_specs=[pl.BlockSpec(memory_space=pltpu.VMEM)] * 2,
        scratch_shapes=[
            pltpu.VMEM((2 * BS, 16 * BS), f32),
            pltpu.VMEM((2, 4, BS, BS), f32),
            pltpu.VMEM((3, BS, BS), f32),
            pltpu.VMEM((2, BS, BS), f32),
            pltpu.VMEM((2, BS, BS), f32),
            pltpu.SemaphoreType.DMA((16,)),
            pltpu.SemaphoreType.DMA((4,)),
            pltpu.SemaphoreType.DMA((2, 4, 2)),
            pltpu.SemaphoreType.DMA((2, 4)),
            pltpu.SemaphoreType.DMA((3, NX + NY - 1)),
            pltpu.SemaphoreType.DMA((3,)),
            pltpu.SemaphoreType.DMA((QUARTERS, PIECES, 3)),
            pltpu.SemaphoreType.DMA((QUARTERS, PIECES, 2)),
        ],
        compiler_params=pltpu.CompilerParams(
            collective_id=0, has_side_effects=True, vmem_limit_bytes=24 * 1024 * 1024
        ),
        name="panels",
    )(kernel)
    return pl.pallas_call(
        update_kernel,
        grid=(4,),
        out_shape=jax.ShapeDtypeStruct(kernel.shape, f32),
        in_specs=[
            pl.BlockSpec((1, BS, 16, BS), lambda i: (i, 0, 0, 0)),
            pl.BlockSpec((1, BS, 2 * BS), lambda i: (i, 0, 0)),
            pl.BlockSpec((2 * BS, 16 * BS), lambda i: (0, 0)),
        ],
        out_specs=pl.BlockSpec((1, BS, 16, BS), lambda i: (i, 0, 0, 0)),
        compiler_params=pltpu.CompilerParams(vmem_limit_bytes=32 * 1024 * 1024),
        name="update",
    )(kernel, pr, pc)


def solution(mesh):
    spec = P(None, "row", None, "col")
    return jax.shard_map(shards, mesh=mesh, in_specs=(spec,), out_specs=spec, check_vma=False)
```

time: 572 us -> 290 us (0.51)
  the two profiles are of different devices: /device:TPU:128 before, /device:TPU:162 now
where the time goes in v1:
time: 290 us
  Pallas kernels  288 us (99%)
    pallas_call x1, Pallas kernels, shards(): pl.pallas_call(panels_kernel, out_shape=[jax.ShapeDtypeStruct((4, BS, 2 *...  276 us
    pallas_call x1, Pallas kernels, shards(): pl.pallas_call(update_kernel, grid=(4,), out_shape=jax.ShapeDtypeStruct(k...  11.8 us

profile of v1, /device:TPU:162, one launch (start us, length us, event | category | flops | bytes accessed | tf_op | source)
XLA Modules:
  0.0 290.3 jit_solution(9475736233946340171)
XLA Ops:
  0.0 0.0 copy-start
  0.0 2.2 copy-done
  2.2 0.0 copy-start.1
  2.2 276.2 %panels.1 = (f32[4,128,256]{2,1,0:T(8,128)S(1)}, f32[256,2048]{1,0:T(8,128)S(1)}) custom-call(f32[4,128,16,128]{3,2,1,0:T(8,128)S(1)} %copy-done), custom_call_target="tpu_custom_call" | custom-call | tf_op jit(solution)/shard_map/panels/pallas_call | solution.py:400
  278.4 0.0 copy-done.1
  278.4 11.8 %update.1 = f32[4,128,16,128]{3,2,1,0:T(8,128)} custom-call(f32[4,128,16,128]{3,2,1,0:T(8,128)S(1)} %copy-done.1, f32[4,128,256]{2,1,0:T(8,128)S(1)} %get-tuple-element.7.pr_ref, f32[256,2048]{1,0:T(8,128)S(1)} %get-tuple-element.8.pc_ref), custom_call_target="tpu_custom_call" | custom-call | tf_op jit(solution)/shard_map/update/pallas_call | solution.py:425
Async XLA Ops:
  0.0 2.2 copy-start
  2.2 276.2 %copy-start.1 = (f32[4,128,16,128]{3,2,1,0:T(8,128)S(1)}, f32[4,128,16,128]{3,2,1,0:T(8,128)}, u32[]{:S(2)}) copy-start(f32[4,128,16,128]{3,2,1,0:T(8,128)} %a_ref.3) | copy-start | bytes 12582916

commit v2 on v1

v2 whole, which is shorter than its diff:
```python
import jax
import jax.numpy as jnp
from jax import lax
from jax.experimental import pallas as pl
from jax.experimental.pallas import tpu as pltpu
from jax.sharding import PartitionSpec as P

NX, NY, NZ = 4, 4, 8
BS = 128
GROUP = 8
GROUPS = BS // GROUP
QUARTERS = 4
PIECES = 4
MESH = pl.DeviceIdType.MESH


def dot_nn(a, b):
    return lax.dot_general(
        a,
        b,
        (((1,), (0,)), ((), ())),
        precision=lax.Precision.HIGHEST,
        preferred_element_type=jnp.float32,
    )


def dot_nt(a, b):
    return lax.dot_general(
        a,
        b,
        (((1,), (1,)), ((), ())),
        precision=lax.Precision.HIGHEST,
        preferred_element_type=jnp.float32,
    )


def split(value):
    high = value.astype(jnp.bfloat16)
    return high, (value - high.astype(jnp.float32)).astype(jnp.bfloat16)


def dot3(a, b, over):
    def one(p, q):
        return lax.dot_general(p, q, (((1,), (over,)), ((), ())), preferred_element_type=jnp.float32)

    return one(a[0], b[0]) + (one(a[1], b[0]) + one(a[0], b[1]))


def lane(value, index):
    return jnp.broadcast_to(value[:, index : index + 1], (GROUP, BS))


def factor_block(block, upper_ref, inverse_ref, hook):
    rows = lax.broadcasted_iota(jnp.int32, (GROUP, BS), 0)
    cols = lax.broadcasted_iota(jnp.int32, (GROUP, BS), 1)
    left = [block[GROUP * g : GROUP * (g + 1), :] for g in range(GROUPS)]
    right = [jnp.where(cols == rows + GROUP * g, 1.0, 0.0).astype(jnp.float32) for g in range(GROUPS)]
    for k in range(GROUPS):
        hook(k)
        base = GROUP * k
        r = [jnp.broadcast_to(left[k][i : i + 1, :], (GROUP, BS)) for i in range(GROUP)]
        q = [jnp.broadcast_to(right[k][i : i + 1, :], (GROUP, BS)) for i in range(GROUP)]
        d = [[lane(r[i], base + j) if j <= i else None for j in range(GROUP)] for i in range(GROUP)]
        c = [[lane(left[g], base + p) for p in range(GROUP)] for g in range(k + 1, GROUPS)]
        inv = [None] * GROUP
        for p in range(GROUP):
            inv[p] = lax.rsqrt(d[p][p])
            for i in range(p + 1, GROUP):
                d[i][p] = d[i][p] * inv[p]
            r[p] = r[p] * inv[p]
            q[p] = q[p] * inv[p]
            for i in range(p + 1, GROUP):
                for j in range(p + 1, i + 1):
                    d[i][j] = d[i][j] - d[i][p] * d[j][p]
                r[i] = r[i] - d[i][p] * r[p]
                q[i] = q[i] - d[i][p] * q[p]
            if k + 1 < GROUPS:
                first = c[0]
                first[p] = first[p] * inv[p]
                for j in range(p + 1, GROUP):
                    first[j] = first[j] - first[p] * d[j][p]
                left[k + 1] = left[k + 1] - first[p] * r[p]
                right[k + 1] = right[k + 1] - first[p] * q[p]
        for p in range(GROUP):
            at = base + p
            upper_ref[at : at + 1, :] = jnp.where(cols[0:1] >= at, r[p][0:1], 0.0)
            inverse_ref[at : at + 1, :] = q[p][0:1]
        if k + 2 < GROUPS:
            v = [None] * GROUP
            w = [None] * GROUP
            for p in range(GROUP - 1, -1, -1):
                a, b = r[p], q[p]
                for s in range(p + 1, GROUP):
                    a = a - d[s][p] * v[s]
                    b = b - d[s][p] * w[s]
                v[p] = a * inv[p]
                w[p] = b * inv[p]
            for g in range(k + 2, GROUPS):
                mult = c[g - k - 1]
                for p in range(GROUP):
                    left[g] = left[g] - mult[p] * v[p]
                    right[g] = right[g] - mult[p] * w[p]


def remote(src, dst, send, recv, target):
    return pltpu.make_async_remote_copy(
        src_ref=src, dst_ref=dst, send_sem=send, recv_sem=recv, device_id=target, device_id_type=MESH
    )


def panels_kernel(
    a_ref,
    pr_high,
    pr_low,
    pc_high,
    pc_low,
    own,
    flat,
    cbuf,
    rbuf,
    corner,
    upper,
    inverse,
    load_c,
    load_r,
    load_a,
    r_send,
    r_recv,
    k_send,
    k_recv,
    c_send,
    c_recv,
):
    grid_row = lax.axis_index("row")
    z = lax.axis_index("col")
    core = lax.rem(grid_row, 2)
    y = lax.rem(grid_row // 2, NY)
    x = grid_row // (2 * NY)

    def at(i, j, core_, z_):
        return ((lax.rem(i, NX) * NY + lax.rem(j, NY)) * 2 + core_, lax.rem(z_, NZ))

    sibling = at(x, y, 1 - core, z)
    root = (x == 0) & (y == 0)
    mine = pl.multiple_of(core * BS, BS)

    barrier = pltpu.get_barrier_semaphore()
    near = [at(x + m, y, core, z) for m in range(1, NX)]
    near += [at(x, y + m, core, z) for m in range(1, NY)]
    near += [at(x, y, core, z + m) for m in range(1, NZ)] + [sibling]
    for target in near:
        pl.semaphore_signal(barrier, inc=1, device_id=target, device_id_type=MESH)

    def c_load(j):
        return pltpu.make_async_copy(
            a_ref.at[0, :, j, :], cbuf.at[pl.ds(mine, BS), pl.ds(j * BS, BS)], load_c.at[j]
        )

    def r_load(panel, i):
        return pltpu.make_async_copy(a_ref.at[i, :, 0, :], rbuf.at[panel, i], load_r.at[i])

    def a_load(i, j):
        return pltpu.make_async_copy(a_ref.at[i, :, j, :], flat.at[i, :, pl.ds(j * BS, BS)], load_a.at[i, j])

    for panel in range(2):

        @pl.when(z == panel)
        def _():
            for i in range(4):
                r_load(panel, i).start()

    @pl.when(root)
    def _():
        for j in range(16):
            c_load(j).start()

    for panel in range(2):

        @pl.when(z == panel)
        def _():
            for i in range(4):
                r_load(panel, i).wait()

    @pl.when(root)
    def _():
        for j in range(16):
            c_load(j).wait()

    for i in range(4):
        for j in range(16):
            a_load(i, j).start()

    pl.semaphore_wait(barrier, len(near))

    def r_where(panel):
        rel = lax.rem(z + NZ - panel, NZ)
        return rel == 0, rel <= 3, (rel == 0) | (rel >= 6), jnp.where(rel <= 4, rel, NZ - rel)

    def r_copy(panel, i, up):
        step = 1 if up else NZ - 1
        return remote(
            rbuf.at[panel, i],
            rbuf.at[panel, i],
            r_send.at[panel, i, 0 if up else 1],
            r_recv.at[panel, i],
            at(x, y, core, z + step),
        )

    def r_relay(slot):
        for panel in range(2):
            first, up, down, depth = r_where(panel)
            i = slot - depth
            live = (i >= 0) & (i < 4)

            @pl.when(live & jnp.logical_not(first))
            def _():
                r_copy(panel, i, True).wait_recv()

            @pl.when(live & up)
            def _():
                r_copy(panel, i, True).start()

            @pl.when(live & down)
            def _():
                r_copy(panel, i, False).start()

    def r_finish(panel, i):
        _, up, down, _ = r_where(panel)

        @pl.when(up)
        def _():
            r_copy(panel, i, True).wait_send()

        @pl.when(down)
        def _():
            r_copy(panel, i, False).wait_send()

    owners = (0, 1, 1)
    planes = (0, 0, 1)

    def k_copy(block, slot, target):
        return remote(corner.at[block], corner.at[block], k_send.at[block, slot], k_recv.at[block], target)

    def k_sends(block):
        owner = core == owners[block]
        source = owner & root & (z == planes[block])
        stages = [(source, [k_copy(block, m - 1, at(x, y, core, z + m)) for m in range(1, NZ)])]
        stages.append((owner & root, [k_copy(block, 6 + m, at(x + m, y, core, z)) for m in range(1, NX)]))
        stages.append((owner & (y == 0), [k_copy(block, 9 + m, at(x, y + m, core, z)) for m in range(1, NY)]))
        stages.append((owner, [k_copy(block, 13, sibling)]))
        return source, stages

    def k_relay(block):
        source, stages = k_sends(block)

        @pl.when(source)
        def _():
            corner[block] = rbuf[planes[block], 0]

        @pl.when(jnp.logical_not(source))
        def _():
            k_copy(block, 0, sibling).wait_recv()

        for cond, copies in stages:

            @pl.when(cond)
            def _(copies=copies):
                for copy in copies:
                    copy.start()

    def k_finish(block):
        for cond, copies in k_sends(block)[1]:

            @pl.when(cond)
            def _(copies=copies):
                for copy in copies:
                    copy.wait_send()

    def c_where(quarter):
        flip = quarter % 2
        a, b = (x, y) if quarter < 2 else (y, x)
        if flip:
            a, b = lax.rem(NX - a, NX), lax.rem(NY - b, NY)
        step = NX - 1 if flip else 1
        along, across = ((step, 0), (0, step)) if quarter < 2 else ((0, step), (step, 0))
        send_along = ((b == 0) & (a < 3)) | ((b > 0) & (a == 3))
        send_across = (a > 0) & (b < 3)
        depth = jnp.where((a == 0) & (b > 0), 4 + b, a + b)
        return (
            send_along,
            at(x + along[0], y + along[1], core, z),
            send_across,
            at(x + across[0], y + across[1], core, z),
            depth,
        )

    def c_rows(quarter, piece, base):
        height = BS // QUARTERS // PIECES
        return pl.ds(pl.multiple_of(base + (quarter * PIECES + piece) * height, height), height)

    def c_copy(quarter, piece, slot, target):
        view = cbuf.at[c_rows(quarter, piece, mine)]
        return remote(view, view, c_send.at[quarter, piece, slot], c_recv.at[quarter, piece, 0], target)

    def c_pair(quarter, piece):
        view = cbuf.at[c_rows(quarter, piece, mine)]
        return remote(view, view, c_send.at[quarter, piece, 2], c_recv.at[quarter, piece, 1], sibling)

    def c_pair_in(quarter, piece):
        view = cbuf.at[c_rows(quarter, piece, BS - mine)]
        return remote(view, view, c_send.at[quarter, piece, 2], c_recv.at[quarter, piece, 1], sibling)

    def c_relay(slot):
        for quarter in range(QUARTERS):
            send_along, along, send_across, across, depth = c_where(quarter)
            piece = slot - depth

            @pl.when((piece >= 0) & (piece < PIECES))
            def _():
                @pl.when(jnp.logical_not(root))
                def _():
                    c_copy(quarter, piece, 0, sibling).wait_recv()

                @pl.when(send_along)
                def _():
                    c_copy(quarter, piece, 0, along).start()

                @pl.when(send_across)
                def _():
                    c_copy(quarter, piece, 1, across).start()

                c_pair(quarter, piece).start()

    def c_finish(quarter, piece):
        send_along, along, send_across, across, _ = c_where(quarter)

        @pl.when(send_along)
        def _():
            c_copy(quarter, piece, 0, along).wait_send()

        @pl.when(send_across)
        def _():
            c_copy(quarter, piece, 1, across).wait_send()

        c_pair(quarter, piece).wait_send()

    k_relay(0)
    c_relay(0)
    r_relay(0)
    c_relay(1)
    r_relay(1)
    k_relay(1)
    k_relay(2)
    pending = []
    for slot in range(2, 7 + PIECES):
        pending.append((c_relay, slot))
        if slot < 8:
            pending.append((r_relay, slot))

    def run(count):
        for _ in range(count):
            if pending:
                f, slot = pending.pop(0)
                f(slot)

    factor_block(corner[0], upper.at[0], inverse.at[0], lambda k: run(1))
    below = dot_nt(corner[1], inverse[0])
    second = corner[2] - dot_nt(below, below)
    factor_block(second, upper.at[1], inverse.at[1], lambda k: run(1))
    run(len(pending))

    first_inverse, second_inverse, below_pair = split(inverse[0]), split(inverse[1]), split(below)

    def keep(i, panel, rows):
        part = slice(panel * BS, (panel + 1) * BS)
        high, low = split(rows)
        pr_high[i, :, part] = high
        pr_low[i, :, part] = low

        @pl.when(z == panel)
        def _():
            own[i] = rows

    for i in range(4):
        first_rows = dot3(split(rbuf[0, i]), first_inverse, 1)
        keep(i, 0, first_rows)
        rest = rbuf[1, i] - dot3(split(first_rows), below_pair, 1)
        keep(i, 1, dot3(split(rest), second_inverse, 1))

    @pl.when((grid_row == 0) & (z == 0))
    def _():
        own[0] = upper[0].T

    @pl.when((grid_row == 0) & (z == 1))
    def _():
        own[0] = jnp.zeros((BS, BS), jnp.float32)

    @pl.when((grid_row == 1) & (z == 1))
    def _():
        own[0] = upper[1].T

    for quarter in range(QUARTERS):
        for piece in range(PIECES):
            c_pair_in(quarter, piece).wait_recv()
    for j in range(4):
        part = pl.ds(j * 512, 512)
        top = split(dot3(first_inverse, split(cbuf[0:BS, part]), 0))
        pc_high[0:BS, part], pc_low[0:BS, part] = top
        rest = cbuf[BS : 2 * BS, part] - dot3(below_pair, top, 0)
        low_half = split(dot3(second_inverse, split(rest), 0))
        pc_high[BS : 2 * BS, part], pc_low[BS : 2 * BS, part] = low_half

    for i in range(4):
        for panel in range(2):
            r_finish(panel, i)
    for block in range(3):
        k_finish(block)
    for quarter in range(QUARTERS):
        for piece in range(PIECES):
            c_finish(quarter, piece)
    for i in range(4):
        for j in range(16):
            a_load(i, j).wait()


def update_kernel(flat, pr_high, pr_low, pc_high, pc_low, own, out_ref, tiles, store):
    grid_row = lax.axis_index("row")
    z = lax.axis_index("col")
    wide = 4

    def out_copy(i):
        return pltpu.make_async_copy(tiles.at[i], out_ref.at[i], store.at[i])

    for i in range(4):
        for j in range(0, 16, wide):
            part = slice(j * BS, (j + wide) * BS)
            rows = (pr_high[i], pr_low[i])
            new = flat[i, :, part] - dot3(rows, (pc_high[:, part], pc_low[:, part]), 0)
            for m in range(wide):
                tiles[i, :, j + m, :] = new[:, m * BS : (m + 1) * BS]
        if i == 0:

            @pl.when(grid_row < 2)
            def _():
                tiles[0] = jnp.zeros((BS, 16, BS), jnp.float32)

        @pl.when(z < 2)
        def _():
            tiles[i, :, 0, :] = own[i]

        out_copy(i).start()
    for i in range(4):
        out_copy(i).wait()


def shards(kernel):
    f32, bf16 = jnp.float32, jnp.bfloat16
    vmem = pl.BlockSpec(memory_space=pltpu.VMEM)
    *factors, flat = pl.pallas_call(
        panels_kernel,
        out_shape=[
            jax.ShapeDtypeStruct((4, BS, 2 * BS), bf16),
            jax.ShapeDtypeStruct((4, BS, 2 * BS), bf16),
            jax.ShapeDtypeStruct((2 * BS, 16 * BS), bf16),
            jax.ShapeDtypeStruct((2 * BS, 16 * BS), bf16),
            jax.ShapeDtypeStruct((4, BS, BS), f32),
            jax.ShapeDtypeStruct((4, BS, 16 * BS), f32),
        ],
        in_specs=[pl.BlockSpec(memory_space=pltpu.HBM)],
        out_specs=[vmem] * 6,
        scratch_shapes=[
            pltpu.VMEM((2 * BS, 16 * BS), f32),
            pltpu.VMEM((2, 4, BS, BS), f32),
            pltpu.VMEM((3, BS, BS), f32),
            pltpu.VMEM((2, BS, BS), f32),
            pltpu.VMEM((2, BS, BS), f32),
            pltpu.SemaphoreType.DMA((16,)),
            pltpu.SemaphoreType.DMA((4,)),
            pltpu.SemaphoreType.DMA((4, 16)),
            pltpu.SemaphoreType.DMA((2, 4, 2)),
            pltpu.SemaphoreType.DMA((2, 4)),
            pltpu.SemaphoreType.DMA((3, 14)),
            pltpu.SemaphoreType.DMA((3,)),
            pltpu.SemaphoreType.DMA((QUARTERS, PIECES, 3)),
            pltpu.SemaphoreType.DMA((QUARTERS, PIECES, 2)),
        ],
        compiler_params=pltpu.CompilerParams(
            collective_id=0, has_side_effects=True, vmem_limit_bytes=44 * 1024 * 1024
        ),
        name="panels",
    )(kernel)
    return pl.pallas_call(
        update_kernel,
        out_shape=jax.ShapeDtypeStruct(kernel.shape, f32),
        in_specs=[vmem] * 6,
        out_specs=pl.BlockSpec(memory_space=pltpu.HBM),
        scratch_shapes=[pltpu.VMEM((4, BS, 16, BS), f32), pltpu.SemaphoreType.DMA((4,))],
        compiler_params=pltpu.CompilerParams(vmem_limit_bytes=32 * 1024 * 1024),
        name="update",
    )(flat, *factors)


def solution(mesh):
    spec = P(None, "row", None, "col")
    return jax.shard_map(shards, mesh=mesh, in_specs=(spec,), out_specs=spec, check_vma=False)
```

time: 290 us -> 71.6 us (0.25)
  the two profiles are of different devices: /device:TPU:162 before, /device:TPU:2 now
where the time goes in v2:
time: 71.6 us; the launch traced here: 71.5 us
  Pallas kernels  71.3 us (100%)
    pallas_call x1, Pallas kernels, shards(): pl.pallas_call(panels_kernel, out_shape=[jax.ShapeDtypeStruct((4, BS, 2 *...  66.2 us
    pallas_call x1, Pallas kernels, shards(): pl.pallas_call(update_kernel, out_shape=jax.ShapeDtypeStruct(kernel.shape...  5.12 us

profile of v2, /device:TPU:2, one launch (start us, length us, event | category | flops | bytes accessed | tf_op | source)
XLA Modules:
  0.0 71.5 jit_solution(7228420528331669100)
XLA Ops:
  0.0 66.2 %panels.1 = (bf16[4,128,256]{2,1,0:T(8,128)(2,1)S(1)}, bf16[4,128,256]{2,1,0:T(8,128)(2,1)S(1)}, bf16[256,2048]{1,0:T(8,128)(2,1)S(1)}, bf16[256,2048]{1,0:T(8,1...) custom-call(f32[4,128,16,128]{3,2,1,0:T(8,128)} %a_ref.1), custom_call_target="tpu_custom_call" | custom-call | tf_op jit(solution)/shard_map/panels/pallas_call | solution.py:459
  66.2 5.1 %update.1 = f32[4,128,16,128]{3,2,1,0:T(8,128)} custom-call(f32[4,128,2048]{2,1,0:T(8,128)S(1)} %get-tuple-element.11.flat, bf16[4,128,256]{2,1,0:T(8,128)(2,1)S(1)} %get-tuple-element.12.pr_high, bf16[4,128,256]{2,1,0:T(8,128)(2,1)S(1)} %get-tuple-element.13.pr_low, bf16[256,2048]{1,0:T(8,128)(2,1)S(1)} %get-tuple-element.14.pc_high, ...), custom_call_target="tpu_custom_call" | custom-call | tf_op jit(solution)/shard_map/update/pallas_call | solution.py:492

commit v3 on v2

--- a/solution.py
+++ b/solution.py
@@ -10,7 +10,37 @@
 GROUP = 8
 GROUPS = BS // GROUP
 QUARTERS = 4
-PIECES = 4
+PIECES = 8
+C_LAG = 4
+STEPS = ((1, 0), (0, 1), (NX - 1, 0), (0, NY - 1))
+CHILDREN = {
+    (0, 0): (0,),
+    (1, 0): (0, 1, 3),
+    (2, 0): (3, 0),
+    (1, 1): (1, 2, 0),
+    (1, 3): (2,),
+    (2, 1): (0,),
+    (2, 3): (3, 0),
+    (1, 2): (2,),
+    (2, 2): (0,),
+}
+
+
+def tree_depths():
+    depths = {(0, 0): 0}
+    todo = [(0, 0)]
+    while todo:
+        a, b = todo.pop()
+        for d in CHILDREN.get((a, b), ()):
+            child = ((a + STEPS[d][0]) % NX, (b + STEPS[d][1]) % NY)
+            depths[child] = depths[(a, b)] + 1
+            todo.append(child)
+    return depths
+
+
+DEPTHS = tree_depths()
+assert len(DEPTHS) == NX * NY
+DEEPEST = max(DEPTHS.values())
 MESH = pl.DeviceIdType.MESH
 
 
@@ -130,6 +160,8 @@
     k_recv,
     c_send,
     c_recv,
+    w_send,
+    w_recv,
 ):
     grid_row = lax.axis_index("row")
     z = lax.axis_index("col")
@@ -147,9 +179,15 @@
     barrier = pltpu.get_barrier_semaphore()
     near = [at(x + m, y, core, z) for m in range(1, NX)]
     near += [at(x, y + m, core, z) for m in range(1, NY)]
-    near += [at(x, y, core, z + m) for m in range(1, NZ)] + [sibling]
+    near += [at(x, y, core, z + m) for m in (1, 2, NZ - 2, NZ - 1)] + [sibling]
+    line = [at(x, y, core, z + m) for m in range(3, NZ - 2)]
     for target in near:
         pl.semaphore_signal(barrier, inc=1, device_id=target, device_id_type=MESH)
+
+    @pl.when(root)
+    def _():
+        for target in line:
+            pl.semaphore_signal(barrier, inc=1, device_id=target, device_id_type=MESH)
 
     def c_load(j):
         return pltpu.make_async_copy(
@@ -186,54 +224,61 @@
         for j in range(16):
             c_load(j).wait()
 
-    for i in range(4):
+    def a_open(i):
         for j in range(16):
             a_load(i, j).start()
 
-    pl.semaphore_wait(barrier, len(near))
-
-    def r_where(panel):
+    @pl.when(root)
+    def _():
+        pl.semaphore_wait(barrier, len(near) + len(line))
+
+    @pl.when(jnp.logical_not(root))
+    def _():
+        pl.semaphore_wait(barrier, len(near))
+
+    def r_copy(panel, i, slot, target):
+        view = rbuf.at[panel, i]
+        return remote(view, view, r_send.at[panel, i, slot], r_recv.at[panel, i], target)
+
+    def r_sends(panel, i):
         rel = lax.rem(z + NZ - panel, NZ)
-        return rel == 0, rel <= 3, (rel == 0) | (rel >= 6), jnp.where(rel <= 4, rel, NZ - rel)
-
-    def r_copy(panel, i, up):
-        step = 1 if up else NZ - 1
-        return remote(
-            rbuf.at[panel, i],
-            rbuf.at[panel, i],
-            r_send.at[panel, i, 0 if up else 1],
-            r_recv.at[panel, i],
-            at(x, y, core, z + step),
-        )
-
-    def r_relay(slot):
+        up, up2, down, down2 = [
+            r_copy(panel, i, slot, at(x, y, core, z + m)) for slot, m in enumerate((1, 2, NZ - 1, NZ - 2))
+        ]
+        return [(rel == 0, (up2, down2, up, down)), (rel == 2, (up2, up)), (rel == NZ - 2, (down,))]
+
+    def r_open(panel, i):
+        cond, copies = r_sends(panel, i)[0]
+
+        @pl.when(cond)
+        def _():
+            for copy in copies:
+                copy.start()
+
+    def r_relay(i):
         for panel in range(2):
-            first, up, down, depth = r_where(panel)
-            i = slot - depth
-            live = (i >= 0) & (i < 4)
-
-            @pl.when(live & jnp.logical_not(first))
-            def _():
-                r_copy(panel, i, True).wait_recv()
-
-            @pl.when(live & up)
-            def _():
-                r_copy(panel, i, True).start()
-
-            @pl.when(live & down)
-            def _():
-                r_copy(panel, i, False).start()
+            for cond, copies in r_sends(panel, i)[1:]:
+
+                @pl.when(cond)
+                def _(copies=copies):
+                    copies[0].wait_recv()
+                    for copy in copies:
+                        copy.start()
+
+    def r_arrived(panel, i):
+        rel = lax.rem(z + NZ - panel, NZ)
+
+        @pl.when((rel != 0) & (rel != 2) & (rel != NZ - 2))
+        def _():
+            r_copy(panel, i, 0, sibling).wait_recv()
 
     def r_finish(panel, i):
-        _, up, down, _ = r_where(panel)
-
-        @pl.when(up)
-        def _():
-            r_copy(panel, i, True).wait_send()
-
-        @pl.when(down)
-        def _():
-            r_copy(panel, i, False).wait_send()
+        for cond, copies in r_sends(panel, i):
+
+            @pl.when(cond)
+            def _(copies=copies):
+                for copy in copies:
+                    copy.wait_send()
 
     owners = (0, 1, 1)
     planes = (0, 0, 1)
@@ -245,23 +290,26 @@
         owner = core == owners[block]
         source = owner & root & (z == planes[block])
         stages = [(source, [k_copy(block, m - 1, at(x, y, core, z + m)) for m in range(1, NZ)])]
-        stages.append((owner & root, [k_copy(block, 6 + m, at(x + m, y, core, z)) for m in range(1, NX)]))
-        stages.append((owner & (y == 0), [k_copy(block, 9 + m, at(x, y + m, core, z)) for m in range(1, NY)]))
-        stages.append((owner, [k_copy(block, 13, sibling)]))
+        stages.append((owner, [k_copy(block, NZ - 1, sibling)]))
         return source, stages
+
+    def k_open(block):
+        source, stages = k_sends(block)
+
+        @pl.when(source)
+        def _():
+            corner[block] = rbuf[planes[block], 0]
+            for copy in stages[0][1]:
+                copy.start()
 
     def k_relay(block):
         source, stages = k_sends(block)
 
-        @pl.when(source)
-        def _():
-            corner[block] = rbuf[planes[block], 0]
-
         @pl.when(jnp.logical_not(source))
         def _():
             k_copy(block, 0, sibling).wait_recv()
 
-        for cond, copies in stages:
+        for cond, copies in stages[1:]:
 
             @pl.when(cond)
             def _(copies=copies):
@@ -277,43 +325,46 @@
                     copy.wait_send()
 
     def c_where(quarter):
-        flip = quarter % 2
-        a, b = (x, y) if quarter < 2 else (y, x)
-        if flip:
-            a, b = lax.rem(NX - a, NX), lax.rem(NY - b, NY)
-        step = NX - 1 if flip else 1
-        along, across = ((step, 0), (0, step)) if quarter < 2 else ((0, step), (step, 0))
-        send_along = ((b == 0) & (a < 3)) | ((b > 0) & (a == 3))
-        send_across = (a > 0) & (b < 3)
-        depth = jnp.where((a == 0) & (b > 0), 4 + b, a + b)
-        return (
-            send_along,
-            at(x + along[0], y + along[1], core, z),
-            send_across,
-            at(x + across[0], y + across[1], core, z),
-            depth,
-        )
-
-    def c_rows(quarter, piece, base):
-        height = BS // QUARTERS // PIECES
-        return pl.ds(pl.multiple_of(base + (quarter * PIECES + piece) * height, height), height)
+        a, b = ((x, y), (y, NX - x), (NX - x, NY - y), (NY - y, x))[quarter]
+        place = lax.rem(a, NX) * NY + lax.rem(b, NY)
+        depth = jnp.int32(0)
+        for (i, j), value in DEPTHS.items():
+            depth = jnp.where(place == i * NY + j, value, depth)
+        edges = []
+        for d in range(4):
+            cond = None
+            for (i, j), children in CHILDREN.items():
+                if d in children:
+                    here = place == i * NY + j
+                    cond = here if cond is None else cond | here
+            if cond is not None:
+                step = STEPS[(d + quarter) % 4]
+                edges.append((cond, at(x + step[0], y + step[1], core, z)))
+        return depth, edges
+
+    c_tree = [c_where(quarter) for quarter in range(QUARTERS)]
+
+    def c_view(quarter, piece, base):
+        rows = pl.multiple_of(base + (quarter * (PIECES // 2) + piece // 2) * GROUP, GROUP)
+        cols = pl.multiple_of(lax.rem(piece, 2) * (8 * BS), 8 * BS)
+        return cbuf.at[pl.ds(rows, GROUP), pl.ds(cols, 8 * BS)]
 
     def c_copy(quarter, piece, slot, target):
-        view = cbuf.at[c_rows(quarter, piece, mine)]
+        view = c_view(quarter, piece, mine)
         return remote(view, view, c_send.at[quarter, piece, slot], c_recv.at[quarter, piece, 0], target)
 
     def c_pair(quarter, piece):
-        view = cbuf.at[c_rows(quarter, piece, mine)]
-        return remote(view, view, c_send.at[quarter, piece, 2], c_recv.at[quarter, piece, 1], sibling)
+        view = c_view(quarter, piece, mine)
+        return remote(view, view, c_send.at[quarter, piece, 4], c_recv.at[quarter, piece, 1], sibling)
 
     def c_pair_in(quarter, piece):
-        view = cbuf.at[c_rows(quarter, piece, BS - mine)]
-        return remote(view, view, c_send.at[quarter, piece, 2], c_recv.at[quarter, piece, 1], sibling)
+        view = c_view(quarter, piece, BS - mine)
+        return remote(view, view, c_send.at[quarter, piece, 4], c_recv.at[quarter, piece, 1], sibling)
 
     def c_relay(slot):
         for quarter in range(QUARTERS):
-            send_along, along, send_across, across, depth = c_where(quarter)
-            piece = slot - depth
+            depth, edges = c_tree[quarter]
+            piece = slot - C_LAG * depth
 
             @pl.when((piece >= 0) & (piece < PIECES))
             def _():
@@ -321,71 +372,141 @@
                 def _():
                     c_copy(quarter, piece, 0, sibling).wait_recv()
 
-                @pl.when(send_along)
-                def _():
-                    c_copy(quarter, piece, 0, along).start()
-
-                @pl.when(send_across)
-                def _():
-                    c_copy(quarter, piece, 1, across).start()
+                for d, (cond, target) in enumerate(edges):
+
+                    @pl.when(cond)
+                    def _():
+                        c_copy(quarter, piece, d, target).start()
 
                 c_pair(quarter, piece).start()
 
     def c_finish(quarter, piece):
-        send_along, along, send_across, across, _ = c_where(quarter)
-
-        @pl.when(send_along)
-        def _():
-            c_copy(quarter, piece, 0, along).wait_send()
-
-        @pl.when(send_across)
-        def _():
-            c_copy(quarter, piece, 1, across).wait_send()
+        for d, (cond, target) in enumerate(c_tree[quarter][1]):
+
+            @pl.when(cond)
+            def _():
+                c_copy(quarter, piece, d, target).wait_send()
 
         c_pair(quarter, piece).wait_send()
 
-    k_relay(0)
-    c_relay(0)
-    r_relay(0)
-    c_relay(1)
-    r_relay(1)
-    k_relay(1)
-    k_relay(2)
-    pending = []
-    for slot in range(2, 7 + PIECES):
-        pending.append((c_relay, slot))
-        if slot < 8:
-            pending.append((r_relay, slot))
-
-    def run(count):
-        for _ in range(count):
-            if pending:
-                f, slot = pending.pop(0)
-                f(slot)
-
-    factor_block(corner[0], upper.at[0], inverse.at[0], lambda k: run(1))
-    below = dot_nt(corner[1], inverse[0])
-    second = corner[2] - dot_nt(below, below)
-    factor_block(second, upper.at[1], inverse.at[1], lambda k: run(1))
-    run(len(pending))
-
-    first_inverse, second_inverse, below_pair = split(inverse[0]), split(inverse[1]), split(below)
-
-    def keep(i, panel, rows):
-        part = slice(panel * BS, (panel + 1) * BS)
-        high, low = split(rows)
-        pr_high[i, :, part] = high
-        pr_low[i, :, part] = low
-
-        @pl.when(z == panel)
-        def _():
-            own[i] = rows
-
+    half = BS // 2
+    a = jnp.where(core == 0, x, y)
+    b = jnp.where(core == 0, y, x)
+
+    def w_at(i, j):
+        return at(jnp.where(core == 0, i, j), jnp.where(core == 0, j, i), core, z)
+
+    def w_view(part):
+        rows = pl.ds(pl.multiple_of(core * half, half), half)
+        return inverse.at[pl.ds(0, 1) if part == 0 else pl.ds(1, 2), rows]
+
+    def w_copy(part, slot, target):
+        return remote(w_view(part), w_view(part), w_send.at[part, slot], w_recv.at[part, 0], target)
+
+    def w_pair(part):
+        return remote(w_view(part), w_view(part), w_send.at[part, 6], w_recv.at[part, 1], sibling)
+
+    def w_sends(part):
+        return [
+            (root, [w_copy(part, m - 1, w_at(a + m, b)) for m in range(1, NX)]),
+            (b == 0, [w_copy(part, 2 + m, w_at(a, b + m)) for m in range(1, NY)]),
+            (jnp.logical_not(root), [w_pair(part)]),
+        ]
+
+    def w_relay(part):
+        @pl.when(jnp.logical_not(root))
+        def _():
+            w_copy(part, 0, sibling).wait_recv()
+
+        for cond, copies in w_sends(part):
+
+            @pl.when(cond)
+            def _(copies=copies):
+                for copy in copies:
+                    copy.start()
+
+    def w_arrived(part):
+        @pl.when(jnp.logical_not(root))
+        def _():
+            w_pair(part).wait_recv()
+
+    def w_finish(part):
+        for cond, copies in w_sends(part):
+
+            @pl.when(cond)
+            def _(copies=copies):
+                for copy in copies:
+                    copy.wait_send()
+
+    last_c = PIECES + DEEPEST * C_LAG
+
+    @pl.when(root)
+    def _():
+        k_open(0)
+        k_open(1)
+        k_open(2)
+        c_relay(0)
+        for i in range(4):
+            for panel in range(2):
+                r_open(panel, i)
+            c_relay(1 + i)
+        k_relay(0)
+        todo = {(0, 1 + i): (c_relay, 5 + i) for i in range(3)}
+        todo |= {(0, 6): (k_relay, 1), (0, 8): (k_relay, 2), (1, 4): (r_relay, 0)}
+        todo |= {(1, 2): (a_open, 0), (1, 6): (a_open, 1), (1, 10): (a_open, 2), (1, 14): (a_open, 3)}
+
+        def hook(panel):
+            def run(k):
+                if (panel, k) in todo:
+                    f, value = todo[panel, k]
+                    f(value)
+
+            return run
+
+        factor_block(corner[0], upper.at[0], inverse.at[0], hook(0))
+        w_relay(0)
+        below = dot_nt(corner[1], inverse[0])
+        second = corner[2] - dot_nt(below, below)
+        through = dot_nn(below, inverse[0])
+        factor_block(second, upper.at[1], inverse.at[2], hook(1))
+        inverse[1] = -dot_nn(inverse[2], through)
+        w_relay(1)
+        for i in range(1, 4):
+            r_relay(i)
+
+    @pl.when(jnp.logical_not(root))
+    def _():
+        for i in range(4):
+            for panel in range(2):
+                r_open(panel, i)
+        relays = {6: 0, 11: 1, 16: 2, 21: 3}
+        for slot in range(last_c):
+            c_relay(slot)
+            if 1 <= slot <= 4:
+                a_open(slot - 1)
+            if slot in relays:
+                r_relay(relays[slot])
+            if slot == last_c - 5:
+                w_relay(0)
+        w_relay(1)
+
+    for panel in range(2):
+        for i in range(4):
+            r_arrived(panel, i)
+    for part in range(2):
+        w_arrived(part)
+
+    zero = jnp.zeros((BS, BS), jnp.float32)
+    top = jnp.concatenate([inverse[0], zero], 1)
+    whole = split(jnp.concatenate([top, jnp.concatenate([inverse[1], inverse[2]], 1)], 0))
     for i in range(4):
-        first_rows = dot3(split(rbuf[0, i]), first_inverse, 1)
-        keep(i, 0, first_rows)
-        rest = rbuf[1, i] - dot3(split(first_rows), below_pair, 1)
-        keep(i, 1, dot3(split(rest), second_inverse, 1))
+        rows = dot3(split(jnp.concatenate([rbuf[0, i], rbuf[1, i]], 1)), whole, 1)
+        pr_high[i], pr_low[i] = split(dot3(split(rows), whole, 0))
+        for panel in range(2):
+
+            @pl.when(z == panel)
+            def _():
+                own[i] = rows[:, panel * BS : (panel + 1) * BS]
 
     @pl.when((grid_row == 0) & (z == 0))
     def _():
@@ -402,19 +523,19 @@
     for quarter in range(QUARTERS):
         for piece in range(PIECES):
             c_pair_in(quarter, piece).wait_recv()
-    for j in range(4):
-        part = pl.ds(j * 512, 512)
-        top = split(dot3(first_inverse, split(cbuf[0:BS, part]), 0))
-        pc_high[0:BS, part], pc_low[0:BS, part] = top
-        rest = cbuf[BS : 2 * BS, part] - dot3(below_pair, top, 0)
-        low_half = split(dot3(second_inverse, split(rest), 0))
-        pc_high[BS : 2 * BS, part], pc_low[BS : 2 * BS, part] = low_half
-
+    pc_high[...], pc_low[...] = split(cbuf[...])
+
+    for part in range(2):
+        w_finish(part)
     for i in range(4):
         for panel in range(2):
             r_finish(panel, i)
-    for block in range(3):
-        k_finish(block)
+
+    @pl.when(root)
+    def _():
+        for block in range(3):
+            k_finish(block)
+
     for quarter in range(QUARTERS):
         for piece in range(PIECES):
             c_finish(quarter, piece)
@@ -473,16 +594,18 @@
             pltpu.VMEM((2, 4, BS, BS), f32),
             pltpu.VMEM((3, BS, BS), f32),
             pltpu.VMEM((2, BS, BS), f32),
-            pltpu.VMEM((2, BS, BS), f32),
+            pltpu.VMEM((3, BS, BS), f32),
             pltpu.SemaphoreType.DMA((16,)),
             pltpu.SemaphoreType.DMA((4,)),
             pltpu.SemaphoreType.DMA((4, 16)),
-            pltpu.SemaphoreType.DMA((2, 4, 2)),
+            pltpu.SemaphoreType.DMA((2, 4, 4)),
             pltpu.SemaphoreType.DMA((2, 4)),
-            pltpu.SemaphoreType.DMA((3, 14)),
+            pltpu.SemaphoreType.DMA((3, NZ)),
             pltpu.SemaphoreType.DMA((3,)),
-            pltpu.SemaphoreType.DMA((QUARTERS, PIECES, 3)),
+            pltpu.SemaphoreType.DMA((QUARTERS, PIECES, 5)),
             pltpu.SemaphoreType.DMA((QUARTERS, PIECES, 2)),
+            pltpu.SemaphoreType.DMA((2, 7)),
+            pltpu.SemaphoreType.DMA((2, 2)),
         ],
         compiler_params=pltpu.CompilerParams(
             collective_id=0, has_side_effects=True, vmem_limit_bytes=44 * 1024 * 1024

time: 71.6 us -> 48.8 us (0.68)
  the two profiles are of different devices: /device:TPU:2 before, /device:TPU:128 now
where the time goes in v3:
time: 48.8 us; the launch traced here: 48.7 us
  Pallas kernels  48.5 us (99%)
    pallas_call x1, Pallas kernels, shards(): pl.pallas_call(panels_kernel, out_shape=[jax.ShapeDtypeStruct((4, BS, 2 *...  43.5 us
    pallas_call x1, Pallas kernels, shards(): pl.pallas_call(update_kernel, out_shape=jax.ShapeDtypeStruct(kernel.shape...  5.04 us

profile of v3, /device:TPU:128, one launch (start us, length us, event | category | flops | bytes accessed | tf_op | source)
XLA Modules:
  0.0 48.7 jit_solution(6836943540098906756)
XLA Ops:
  0.0 43.5 %panels.1 = (bf16[4,128,256]{2,1,0:T(8,128)(2,1)S(1)}, bf16[4,128,256]{2,1,0:T(8,128)(2,1)S(1)}, bf16[256,2048]{1,0:T(8,128)(2,1)S(1)}, bf16[256,2048]{1,0:T(8,1...) custom-call(f32[4,128,16,128]{3,2,1,0:T(8,128)} %a_ref.1), custom_call_target="tpu_custom_call" | custom-call | tf_op jit(solution)/shard_map/panels/pallas_call | solution.py:580
  43.5 5.0 %update.1 = f32[4,128,16,128]{3,2,1,0:T(8,128)} custom-call(f32[4,128,2048]{2,1,0:T(8,128)S(1)} %get-tuple-element.11.flat, bf16[4,128,256]{2,1,0:T(8,128)(2,1)S(1)} %get-tuple-element.12.pr_high, bf16[4,128,256]{2,1,0:T(8,128)(2,1)S(1)} %get-tuple-element.13.pr_low, bf16[256,2048]{1,0:T(8,128)(2,1)S(1)} %get-tuple-element.14.pc_high, ...), custom_call_target="tpu_custom_call" | custom-call | tf_op jit(solution)/shard_map/update/pallas_call | solution.py:615

commit v4 on v3

--- a/solution.py
+++ b/solution.py
@@ -452,7 +452,7 @@
             c_relay(1 + i)
         k_relay(0)
         todo = {(0, 1 + i): (c_relay, 5 + i) for i in range(3)}
-        todo |= {(0, 6): (k_relay, 1), (0, 8): (k_relay, 2), (1, 4): (r_relay, 0)}
+        todo |= {(0, 6): (k_relay, 1), (0, 8): (k_relay, 2), (1, 4): (r_relay, 0), (1, 12): (r_relay, 1)}
         todo |= {(1, 2): (a_open, 0), (1, 6): (a_open, 1), (1, 10): (a_open, 2), (1, 14): (a_open, 3)}
 
         def hook(panel):
@@ -471,7 +471,7 @@
         factor_block(second, upper.at[1], inverse.at[2], hook(1))
         inverse[1] = -dot_nn(inverse[2], through)
         w_relay(1)
-        for i in range(1, 4):
+        for i in range(2, 4):
             r_relay(i)
 
     @pl.when(jnp.logical_not(root))

time: 48.8 us -> 48.8 us (level)
  no operation moved by 1% of the time
where the time goes in v4:
time: 48.8 us; the launch traced here: 48.7 us
  Pallas kernels  48.5 us (99%)
    pallas_call x1, Pallas kernels, shards(): pl.pallas_call(panels_kernel, out_shape=[jax.ShapeDtypeStruct((4, BS, 2 *...  43.5 us
    pallas_call x1, Pallas kernels, shards(): pl.pallas_call(update_kernel, out_shape=jax.ShapeDtypeStruct(kernel.shape...  5.04 us

profile of v4, /device:TPU:128, one launch (start us, length us, event | category | flops | bytes accessed | tf_op | source)
XLA Modules:
  0.0 48.7 jit_solution(7853042086645228931)
XLA Ops:
  0.0 43.5 %panels.1 = (bf16[4,128,256]{2,1,0:T(8,128)(2,1)S(1)}, bf16[4,128,256]{2,1,0:T(8,128)(2,1)S(1)}, bf16[256,2048]{1,0:T(8,128)(2,1)S(1)}, bf16[256,2048]{1,0:T(8,1...) custom-call(f32[4,128,16,128]{3,2,1,0:T(8,128)} %a_ref.1), custom_call_target="tpu_custom_call" | custom-call | tf_op jit(solution)/shard_map/panels/pallas_call | solution.py:580
  43.5 5.0 %update.1 = f32[4,128,16,128]{3,2,1,0:T(8,128)} custom-call(f32[4,128,2048]{2,1,0:T(8,128)S(1)} %get-tuple-element.11.flat, bf16[4,128,256]{2,1,0:T(8,128)(2,1)S(1)} %get-tuple-element.12.pr_high, bf16[4,128,256]{2,1,0:T(8,128)(2,1)S(1)} %get-tuple-element.13.pr_low, bf16[256,2048]{1,0:T(8,128)(2,1)S(1)} %get-tuple-element.14.pc_high, ...), custom_call_target="tpu_custom_call" | custom-call | tf_op jit(solution)/shard_map/update/pallas_call | solution.py:615
